TPU v7x, 32 devices: a whole 2x2x4 slice. The times are simulated.
32 devices in a mesh: tok: 16 (over z, x, core), fsdp: 2 (over y).
Axes of the slice: x: 2, y: 2, z: 4, core: 2. Of those that a mesh axis runs over, the one named last changes fastest.
Arguments:
- qkv: bfloat16 [12288, 3, 3072], P('tok', None, 'fsdp'), may hold values from -42 to 42
- prefix_kv: bfloat16 [2, 2048, 3072], P(None, 'tok', 'fsdp'), may hold values from -9 to 9
- cache_pool: bfloat16 [16, 16, 2, 128, 3072], P('tok', None, None, None, 'fsdp'), may hold values from -9 to 9
- page_table: int32 [16, 16], P('tok'), may hold values from 0 to 15, each once within a row
- cached_lens: int32 [16], P('tok'), may hold values from 0 to 2048, as said below
- span_lens: int32 [16], P('tok'), may hold values from 192 to 768, as said below
- dense_weight: bfloat16 [3072, 6144], P(None, 'fsdp'), may hold values from -0.625 to 0.625
- dense_bias: float32 [6144], P('fsdp'), may hold values from -1.8 to 1.8
Outputs:
- attended: bfloat16 [12288, 6144], P('tok', 'fsdp')
Inputs may be any that keep to these rules, and one draw needn't show every extreme that they name: `page_table`: each row names each of the prompt's 16 stored pages once. `cached_lens`: some prompt has a full cache and some none. `span_lens`: some prompt fills all 768 slots, some a quarter of them.
All inputs are finite; a program needn't handle non-finite values.
Results may differ from a plain program's by a relative error of at most 0.0075.
Values may be sent and summed in bfloat16 or wider, within the bound.
No kernel may reach another device: no remote copies, remote signals or barrier semaphores. Data moves between devices by JAX's collectives and lax.ppermute only.
A program may use at most 320 MiB of HBM per device.

v0:
```python
import functools
import math

import jax
import jax.numpy as jnp
from jax import lax
from jax.experimental import pallas as pl
from jax.experimental.pallas import tpu as pltpu
from jax.sharding import PartitionSpec as P

HD = 96
ROT = 24
LANES = 128
GROUP = 4
GW = GROUP * HD
NEG = -1e30
f32, bf16 = jnp.float32, jnp.bfloat16
SCALE = HD ** -0.5 * math.log2(math.e)
SUM, TOP = HD, HD + 1
STEP = 128
HEAD = 5


def realign(x, h):
    lo = h * HD
    first = lo // LANES * LANES
    off = lo - first
    if off == 0:
        return x[:, first:first + LANES]
    if off + HD <= LANES:
        return pltpu.roll(x[:, first:first + LANES], LANES - off, 1)
    return pltpu.roll(x[:, first:first + 2 * LANES], 2 * LANES - off, 1)[:, :LANES]


def attend_kernel(scal, *rest, local, prefix, send, piece, span, page_len, max_pages, bq, bk):
    it = iter(rest)
    if local:
        qkv, pool, angles = next(it), next(it), next(it)
    else:
        qh, st = next(it), next(it)
    pieces = [next(it) for _ in piece] if prefix else []
    if prefix:
        out = next(it)
    if local:
        qh = next(it)
        if not prefix:
            st = next(it)
        if send:
            qkv_out, pool_out = next(it), next(it)
        qk, sem_q, sem_c = next(it), next(it), next(it)
        if send:
            sem_s, sem_t = next(it), next(it)
    kb, vb, kh, vh = next(it), next(it), next(it), next(it)
    if prefix:
        sem_p = next(it)
    cached = scal[0]
    live = scal[1]
    cols = pl.ds(pl.multiple_of(scal[2], LANES), GW)
    pcol = pl.ds(pl.multiple_of(scal[3], LANES), GW)
    n_pages = pl.cdiv(cached, page_len)
    base_c = span if local else 0
    base_p = span + max_pages * page_len if local else 0
    per = bk // page_len
    n_cb = pl.cdiv(cached, bk)
    n_full = cached // bk
    heads = range(GROUP)
    zero = jnp.zeros((STEP, LANES), bf16)

    def put_v(at, v):
        lane = lax.broadcasted_iota(jnp.int32, (STEP, LANES), 1)
        one = jnp.where(lane == SUM, 1.0, 0.0).astype(bf16)
        for h in heads:
            vh[h, pl.ds(at, STEP), :] = jnp.where(lane < HD, realign(v, h), one)

    def put_k(at, k):
        for h in heads:
            kh[h, pl.ds(at, STEP), :] = realign(k, h)

    if local:
        new_copies = [
            pltpu.make_async_copy(qkv.at[0, :, cols], qk.at[0], sem_q.at[0]),
            pltpu.make_async_copy(qkv.at[1, :, cols], qk.at[1], sem_q.at[1]),
            pltpu.make_async_copy(qkv.at[2, :, cols], vb.at[pl.ds(0, span), :], sem_q.at[2]),
        ]
        for c in new_copies:
            c.start()

        def page_copies(g):
            dst = pl.ds(pl.multiple_of(base_c + g * page_len, page_len), page_len)
            return (pltpu.make_async_copy(pool.at[scal[HEAD + g], 0, :, cols], kb.at[dst, :], sem_c.at[0, g]),
                    pltpu.make_async_copy(pool.at[scal[HEAD + g], 1, :, cols], vb.at[dst, :], sem_c.at[1, g]))

        def start_page(g, c):
            for x in page_copies(g):
                x.start()
            return c
        lax.fori_loop(0, n_pages, start_page, 0)

        if send:
            scol = pl.ds(pl.multiple_of(scal[4], LANES), qkv_out.shape[2])
            qkv_send = pltpu.make_async_copy(qkv.at[:, :, scol], qkv_out, sem_s)
            qkv_send.start()

            def page_send(g):
                page = scal[HEAD + g]
                return pltpu.make_async_copy(pool.at[page, :, :, scol], pool_out.at[page], sem_t.at[g])

            def start_send(g, c):
                page_send(g).start()
                return c
            lax.fori_loop(0, n_pages, start_send, 0)

    def piece_copies(i):
        at, n = piece[i]
        dst = pl.ds(base_p + at, n)
        return (pltpu.make_async_copy(pieces[i].at[0, :, pcol], kb.at[dst, :], sem_p.at[0, i]),
                pltpu.make_async_copy(pieces[i].at[1, :, pcol], vb.at[dst, :], sem_p.at[1, i]))

    if prefix:
        for i in range(len(piece)):
            for x in piece_copies(i):
                x.start()

    if local:
        for c in new_copies:
            c.wait()

        def prep_new(j, c):
            at = pl.multiple_of(j * STEP, STEP)
            r = pl.ds(at, STEP)
            lane = lax.broadcasted_iota(jnp.int32, (STEP, LANES), 1)
            cosine, sine = angles[0, r, :], angles[1, r, :]

            def turn(x, h):
                x = realign(x, h).astype(f32)
                mate = jnp.where(lane < ROT // 2, pltpu.roll(x, LANES - ROT // 2, 1), pltpu.roll(x, ROT // 2, 1))
                x = x * cosine + mate * sine
                return jnp.where(lane < HD, x, 0.0).astype(bf16)
            q, k = qk[0, r, :], qk[1, r, :]
            for h in heads:
                qh[h, r, :] = turn(q, h)
                kh[h, r, :] = turn(k, h)
            put_v(at, vb[r, :])
            return c
        n_new = pl.cdiv(live, STEP)
        lax.fori_loop(0, n_new, prep_new, 0)

        def clear_new(j, c):
            r = pl.ds(pl.multiple_of(j * STEP, STEP), STEP)
            for h in heads:
                vh[h, r, :] = zero
            return c
        lax.fori_loop(n_new, span // STEP, clear_new, 0)

        def prep_page(g, c):
            at = pl.multiple_of(base_c + g * page_len, page_len)

            @pl.when(g < n_pages)
            def _():
                for x in page_copies(g):
                    x.wait()
                put_k(at, kb[pl.ds(at, page_len), :])
                put_v(at, vb[pl.ds(at, page_len), :])

            @pl.when(g >= n_pages)
            def _():
                for h in heads:
                    kh[h, pl.ds(at, page_len), :] = zero
                    vh[h, pl.ds(at, page_len), :] = zero
            return c
        lax.fori_loop(0, n_cb * per, prep_page, 0)

    if prefix:
        for i in range(len(piece)):
            for x in piece_copies(i):
                x.wait()
        total_p = sum(n for _, n in piece)

        def prep_prefix(j, c):
            at = pl.multiple_of(base_p + j * STEP, STEP)
            put_k(at, kb[pl.ds(at, STEP), :])
            put_v(at, vb[pl.ds(at, STEP), :])
            return c
        lax.fori_loop(0, total_p // STEP, prep_prefix, 0)

    def dots(q, h, start, n):
        return lax.dot_general(q, kh[h, pl.ds(start, n), :], (((1,), (1,)), ((), ())), preferred_element_type=f32)

    def fold(state, s, h, start, n):
        top = jnp.max(s, axis=1, keepdims=True)
        new = top if state is None else jnp.maximum(state[0], top)
        p = jnp.exp2((s - new) * SCALE).astype(bf16)
        add = jnp.dot(p, vh[h, pl.ds(start, n), :], preferred_element_type=f32)
        return new, add if state is None else state[1] * jnp.exp2((state[0] - new) * SCALE) + add

    def tile(qt, carry):
        at = pl.multiple_of(qt * bq, bq)
        rows = pl.ds(at, bq)
        qs = [qh[h, rows, :] for h in heads]
        if local:
            seen = lax.broadcasted_iota(jnp.int32, (bq, span), 1) <= lax.broadcasted_iota(jnp.int32, (bq, span), 0) + at
            ss = [dots(q, h, 0, span) for q, h in zip(qs, heads)]
            states = [fold(None, jnp.where(seen, s, NEG), h, 0, span) for s, h in zip(ss, heads)]

            def cache_block(masked, j, sts):
                start = pl.multiple_of(base_c + j * bk, math.gcd(base_c, bk))
                ss = [dots(q, h, start, bk) for q, h in zip(qs, heads)]
                if masked:
                    ok = lax.broadcasted_iota(jnp.int32, (bq, bk), 1) < cached - j * bk
                    ss = [jnp.where(ok, s, NEG) for s in ss]
                return tuple(fold(sx, s, h, start, bk) for sx, s, h in zip(sts, ss, heads))
            states = lax.fori_loop(0, n_full, functools.partial(cache_block, False), tuple(states))
            states = lax.fori_loop(n_full, n_cb, functools.partial(cache_block, True), states)
        else:
            accs = [st[h, rows, :] for h in heads]
            states = [(a[:, TOP:TOP + 1], a) for a in accs]
        if prefix:
            nb = total_p // bk
            for j in range(nb):
                ss = [dots(q, h, base_p + j * bk, bk) for q, h in zip(qs, heads)]
                states = [fold(sx, s, h, base_p + j * bk, bk) for sx, s, h in zip(states, ss, heads)]
            out[rows, :] = jnp.concatenate([(acc / acc[:, SUM:SUM + 1])[:, :HD] for _, acc in states],
                                           axis=1).astype(bf16)
        else:
            lane = lax.broadcasted_iota(jnp.int32, (bq, LANES), 1)
            for h, (m, acc) in zip(heads, states):
                st[h, rows, :] = jnp.where(lane == TOP, m, acc)
        return carry

    lax.fori_loop(0, pl.cdiv(live, bq), tile, 0)

    if send:
        def wait_send(g, c):
            page_send(g).wait()
            return c
        qkv_send.wait()
        lax.fori_loop(0, n_pages, wait_send, 0)


def attend(scal, span, page_len, max_pages, local=None, carry=None, pieces=None, send=0, bq=256):
    info, at = [], 0
    for p in pieces or []:
        info.append((at, p.shape[1]))
        at += p.shape[1]
    bq = math.gcd(span, bq)
    bk = math.gcd(1024, max_pages * page_len) if local else math.gcd(2048, at)
    if local and pieces:
        bk = math.gcd(bk, at)
    keys = (span + max_pages * page_len if local else 0) + at
    any_ = pl.BlockSpec(memory_space=pltpu.HBM)
    smem = pl.BlockSpec(memory_space=pltpu.SMEM)
    vmem = pl.BlockSpec(memory_space=pltpu.VMEM)
    heads = jax.ShapeDtypeStruct((GROUP, span, LANES), bf16)
    state = jax.ShapeDtypeStruct((GROUP, span, LANES), f32)
    args, in_specs, outs, scratch = [scal], [smem], [], []
    if local:
        args += list(local)
        in_specs += [any_, any_, vmem]
    else:
        args += list(carry)
        in_specs += [vmem] * 2
    if pieces:
        args += list(pieces)
        in_specs += [any_] * len(pieces)
        outs.append(jax.ShapeDtypeStruct((span, GW), bf16))
    if local:
        if pieces:
            scratch.append(pltpu.VMEM(heads.shape, bf16))
        else:
            outs += [heads, state]
            if send:
                outs += [jax.ShapeDtypeStruct((3, span, send), bf16),
                         jax.ShapeDtypeStruct((max_pages, 2, page_len, send), bf16)]
        scratch += [
            pltpu.VMEM((2, span, GW), bf16),
            pltpu.SemaphoreType.DMA((3,)),
            pltpu.SemaphoreType.DMA((2, max_pages)),
        ]
        if send:
            scratch += [pltpu.SemaphoreType.DMA, pltpu.SemaphoreType.DMA((max_pages,))]
    scratch += [pltpu.VMEM((keys, GW), bf16)] * 2 + [pltpu.VMEM((GROUP, keys, LANES), bf16)] * 2
    if pieces:
        scratch += [pltpu.SemaphoreType.DMA((2, len(pieces)))]
    res = pl.pallas_call(
        functools.partial(attend_kernel, local=bool(local), prefix=bool(pieces), send=bool(send), piece=info, span=span, page_len=page_len,
                          max_pages=max_pages, bq=bq, bk=bk),
        out_shape=outs,
        in_specs=in_specs,
        out_specs=[vmem] * (len(outs) - 2 * bool(send)) + [any_] * (2 * bool(send)),
        scratch_shapes=scratch,
        compiler_params=pltpu.CompilerParams(vmem_limit_bytes=56 << 20),
        cost_estimate=pl.CostEstimate(flops=8 * span * keys * GROUP * 2 * LANES, bytes_accessed=8 << 20,
                                      transcendentals=span * keys * GROUP),
        name="attend_" + "new" * bool(local) + "prefix" * bool(pieces),
    )(*args)
    return res[0] if pieces else tuple(res)


def project_kernel(scal, *rest, n, bq, depth):
    pieces, w, bias, out, held = rest[:n], rest[n], rest[n + 1], rest[n + 2], rest[n + 3]
    live = scal[0]
    span, cols = out.shape

    @pl.when(pl.program_id(0) == 0)
    def _():
        for i in range(n):
            held[:, pl.ds(pl.multiple_of(scal[1 + i], LANES), depth)] = pieces[i][...]

    for k in range(1, span // bq + 1):
        @pl.when(pl.cdiv(live, bq) == k)
        def _():
            acc = jnp.dot(held[0:k * bq, :], w[...], preferred_element_type=f32) + bias[...]
            ok = lax.broadcasted_iota(jnp.int32, acc.shape, 0) < live
            out[0:k * bq, :] = jnp.where(ok, acc, 0.0).astype(bf16)
            if k * bq < span:
                out[k * bq:span, :] = jnp.zeros((span - k * bq, cols), bf16)


def project(live, offsets, pieces, weight, bias):
    span, depth = pieces[0].shape
    k, cols = weight.shape
    bn = math.gcd(cols, 512)
    n = len(pieces)
    scal = jnp.stack([jnp.asarray(x, jnp.int32) for x in [live] + list(offsets)])
    return pl.pallas_call(
        functools.partial(project_kernel, n=n, bq=math.gcd(span, 256), depth=depth),
        grid=(cols // bn,),
        out_shape=jax.ShapeDtypeStruct((span, cols), bf16),
        in_specs=[pl.BlockSpec(memory_space=pltpu.SMEM)]
        + [pl.BlockSpec((span, depth), lambda j: (0, 0), pipeline_mode=pl.Buffered(1))] * n
        + [pl.BlockSpec((k, bn), lambda j: (0, j)), pl.BlockSpec((1, bn), lambda j: (0, j))],
        out_specs=pl.BlockSpec((span, bn), lambda j: (0, j)),
        scratch_shapes=[pltpu.VMEM((span, k), bf16)],
        compiler_params=pltpu.CompilerParams(vmem_limit_bytes=48 << 20),
        cost_estimate=pl.CostEstimate(flops=2 * span * k * cols, bytes_accessed=2 * (k * cols + span * (k + cols)),
                                      transcendentals=0),
        name="project",
    )(scal, *pieces, weight, bias.reshape(1, cols))


def rotary_angles(positions):
    half = ROT // 2
    inv = jnp.power(10000.0, -jnp.arange(half, dtype=f32) * 2.0 / ROT)
    inv = jnp.concatenate([inv, inv, jnp.zeros(LANES - ROT, f32)])
    ang = positions.astype(f32)[:, None] * inv[None, :]
    sign = jnp.where(jnp.arange(LANES) < half, -1.0, 1.0)
    return jnp.stack([jnp.cos(ang), jnp.sin(ang) * sign])


def chip_ring(chips):
    if chips == 8:
        return [2 * z for z in range(4)] + [2 * z + 1 for z in (3, 2, 1, 0)]
    return list(range(chips))


def order(scal, *firsts):
    for x in firsts:
        scal = scal + (x[(slice(0, 1),) * x.ndim].reshape(()).astype(f32) > 1e30).astype(jnp.int32)
    return scal


def local_fn(qkv, prefix_kv, cache_pool, page_table, cached_lens, span_lens, dense_weight, dense_bias):
    tok, fsdp = lax.axis_size("tok"), lax.axis_size("fsdp")
    span, _, width = qkv.shape
    qkv = jnp.transpose(qkv, (1, 0, 2))
    pool = cache_pool[0]
    max_pages, _, page_len, _ = pool.shape
    prefix_len = prefix_kv.shape[1] * tok
    f = lax.axis_index("fsdp")
    meta = jnp.concatenate([cached_lens, span_lens, page_table[0]])
    rows = jnp.arange(span, dtype=jnp.int32)

    def scalars(m, col, pcol, scol=0):
        return jnp.concatenate([m[:2], jnp.stack([jnp.asarray(x, jnp.int32) for x in (col, pcol, scol)]), m[2:]])

    if width % (2 * GW) or tok % 2 or fsdp != 2:
        table = rotary_angles(prefix_len + meta[0] + rows)
        whole = lax.all_gather(prefix_kv, "tok", axis=1, tiled=True)
        pieces, offsets = [], []
        for g in range(width // GW):
            got = attend(scalars(meta, g * GW, g * GW), span, page_len, max_pages, local=(qkv, pool, table), pieces=[whole])
            every = lax.all_gather(got, "fsdp", axis=0)
            for i in range(fsdp):
                pieces.append(every[i])
                offsets.append(i * width + g * GW)
        return project(meta[1], offsets, pieces, dense_weight, dense_bias)

    half = width // 2
    c = lax.axis_index("tok") % 2
    swap_pairs = [(i, i ^ 1) for i in range(tok)]
    ring = chip_ring(tok // 2)
    n = len(ring)
    ahead = [(2 * ring[i] + k, 2 * ring[(i + 1) % n] + k) for i in range(n) for k in range(2)]
    back = [(b, a) for a, b in ahead]

    def swap(x):
        return lax.ppermute(x, "tok", swap_pairs)

    def part(x, which):
        return lax.dynamic_slice_in_dim(x, which * half, half, x.ndim - 1)

    meta2 = swap(meta)
    mine = jnp.concatenate([part(prefix_kv, c), swap(part(prefix_kv, 1 - c))], axis=1)
    hop = {1: (lax.ppermute(mine, "tok", ahead), lax.ppermute(mine, "tok", back))}
    mates = {0: (meta, qkv, pool, rotary_angles(prefix_len + meta[0] + rows))}
    groups = [g * GW for g in range(half // GW)]
    units = [(who, col) for who in (0, 1) for col in groups]
    steps = n // 2
    carries = {}
    for i, (who, col) in enumerate(units):
        m, a, b, t = mates[who]
        s = scalars(m, col if who else c * half + col, col, (1 - c) * half)
        s = s if i else order(s, mine[:, -1:])
        got = attend(s, span, page_len, max_pages, local=(a, b, t), send=0 if i else half)
        if not i:
            mates[1] = (meta2, swap(got[2]), swap(got[3]), rotary_angles(prefix_len + meta2[0] + rows))
        carries[who, col] = got[:2]
        d = i + 2
        if d <= steps:
            fw, bw = hop[d - 1]
            fw, bw, carries[who, col] = lax.optimization_barrier((fw, bw, carries[who, col]))
            hop[d] = (lax.ppermute(fw, "tok", ahead),)
            if d < steps:
                hop[d] += (lax.ppermute(bw, "tok", back),)
    pieces = [mine] + [x for d in range(1, steps + 1) for x in hop[d]]
    ypairs = [(0, 1), (1, 0)]
    proj, offsets, early = [], [], []
    for who, col in [(w, col) for w in (1, 0) for col in groups]:
        s = scalars(mates[who][0], 0, col)
        s = s if who else order(s, *early)
        got = attend(s, span, page_len, max_pages, carry=carries[who, col], pieces=pieces)
        if who:
            early.append(got)
        far = lax.ppermute(got, "fsdp", ypairs)
        if who:
            got, far = swap(got), swap(far)
        at = (1 - c if who else c) * half + col
        proj += [got, far]
        offsets += [f * width + at, (1 - f) * width + at]
    return project(meta[1], offsets, proj, dense_weight, dense_bias)


def solution(mesh):
    return jax.shard_map(
        local_fn,
        mesh=mesh,
        in_specs=(
            P("tok", None, "fsdp"),
            P(None, "tok", "fsdp"),
            P("tok", None, None, None, "fsdp"),
            P("tok", None),
            P("tok"),
            P("tok"),
            P(None, "fsdp"),
            P("fsdp"),
        ),
        out_specs=P("tok", "fsdp"),
        check_vma=False,
    )
```

profile of v0, /device:TPU:8, one launch (start us, length us, event | category | flops | bytes accessed | tf_op | source)
XLA Modules:
  0.0 521.4 jit_solution(14074906670753578527)
XLA Ops:
  0.0 1.2 constant_dynamic-slice_fusion.1
  2.5 0.7 pad_add_fusion
  3.9 0.7 concatenate.42
  4.7 2.8 multiply_cosine_fusion.1
  7.5 1.0 pad_maximum_fusion.1.rest_2_
  10.3 242.5 %attend_new.4 = (bf16[4,768,128]{2,1,0:T(8,128)(2,1)}, f32[4,768,128]{2,1,0:T(8,128)}, bf16[3,768,768]{2,1,0:T(8,128)(2,1)}, bf16[16,2,128,768]{3,2,1,0:T(8,128)(2,1)}) custom-call(s32[21]{0:T(128)} %broadcast_add_fusion.scal, bf16[3,768,1536]{2,1,0:T(8,128)(2,1)} %bitcast.34, bf16[16,2,128,1536]{3,2,1,0:T(8,128)(2,1)} %bitcast.32, ...), custom_call_target="tpu_custom_call" | custom-call | flops 17716740096 | bytes 8388608 | tf_op jit(solution)/shard_map/attend_new/pallas_call | solution.py:284
  253.4 37.2 %collective-permute-start.2 = (bf16[2,256,768]{2,1,0:T(8,128)(2,1)S(1)}, bf16[2,256,768]{2,1,0:T(8,128)(2,1)S(1)}, u32[]{:S(2)}, u32[]{:S(2)}) collective-permute-start(bf16[2,256,768]{2,1,0:T(8,128)(2,1)S(1)} %pad_maximum_fusion.rest_2_), channel_id=1, source_target_pairs={{0,8},{2,10},{8,16},{10,18},{16,24},{18,26},{24,28},{26,30},{28,20... | collective-permute-start | bytes 2359304 | tf_op jit(solution)/shard_map/ppermute | solution.py:404
  290.6 9.8 %collective-permute-start.3 = (bf16[2,256,768]{2,1,0:T(8,128)(2,1)S(1)}, bf16[2,256,768]{2,1,0:T(8,128)(2,1)}, u32[]{:S(2)}, u32[]{:S(2)}) collective-permute-start(bf16[2,256,768]{2,1,0:T(8,128)(2,1)S(1)} %pad_maximum_fusion.rest_2_), channel_id=1, source_target_pairs={{8,0},{10,2},{16,8},{18,10},{24,16},{26,18},{28,24},{30,26},{20,28... | collective-permute-start | bytes 2359304 | tf_op jit(solution)/shard_map/ppermute | solution.py:404
  300.5 0.7 concatenate.44.scal
  301.3 16.9 %collective-permute-done.2.rest_3_ = bf16[2,256,768]{2,1,0:T(8,128)(2,1)S(1)} collective-permute-done((bf16[2,256,768]{2,1,0:T(8,128)(2,1)S(1)}, bf16[2,256,768]{2,1,0:T(8,128)(2,1)S(1)}, u32[]{:S(2)}, u32[]{:S(2)}) %collective-permute-start.2) | collective-permute-done | bytes 786464 | tf_op jit(solution)/shard_map/ppermute | solution.py:404
  318.2 2.0 collective-permute-start.5
  320.2 25.2 %attend_new.5 = (bf16[4,768,128]{2,1,0:T(8,128)(2,1)}, f32[4,768,128]{2,1,0:T(8,128)}) custom-call(s32[21]{0:T(128)} %concatenate.44.scal, bf16[3,768,1536]{2,1,0:T(8,128)(2,1)} %bitcast.35, bf16[16,2,128,1536]{3,2,1,0:T(8,128)(2,1)} %bitcast.33, f32[2,768,128]{2,1,0:T(8,128)} %pad_maximum_fusion.1.rest_2_), custom_call_target="tpu_custom_call" | custom-call | flops 17716740096 | bytes 8388608 | tf_op jit(solution)/shard_map/attend_new/pallas_call | solution.py:284
  345.5 0.7 concatenate.46.scal
  346.2 0.7 add_add_fusion.2.scal
  346.8 0.7 add_add_fusion.1
  347.5 1.0 pad_maximum_fusion.2.rest_2_
  348.5 5.3 %collective-permute-start.6 = (bf16[2,256,768]{2,1,0:T(8,128)(2,1)}, bf16[2,256,768]{2,1,0:T(8,128)(2,1)S(1)}, u32[]{:S(2)}, u32[]{:S(2)}) collective-permute-start(bf16[2,256,768]{2,1,0:T(8,128)(2,1)} %collective-permute-done.4.rest_5_), channel_id=1, source_target_pairs={{0,8},{2,10},{8,16},{10,18},{16,24},{18,26},{24,28},{26,30},{28,20... | collective-permute-start | bytes 2359304 | tf_op jit(solution)/shard_map/ppermute | solution.py:422
  353.8 25.4 %attend_new.6 = (bf16[4,768,128]{2,1,0:T(8,128)(2,1)}, f32[4,768,128]{2,1,0:T(8,128)}) custom-call(s32[21]{0:T(128)} %get-tuple-element.53.scal, bf16[3,768,768]{2,1,0:T(8,128)(2,1)} %collective-permute-done.8.rest_0_, bf16[16,2,128,768]{3,2,1,0:T(8,128)(2,1)} %collective-permute-done.9.rest_1_, f32[2,768,128]{2,1,0:T(8,128)} %pad_maximum_fusion.2.rest_2_), custom_call_target="tpu_custom_call" | custom-call | flops 17716740096 | bytes 8388608 | tf_op jit(solution)/shard_map/attend_new/pallas_call | solution.py:284
  379.4 26.1 %attend_new.7 = (bf16[4,768,128]{2,1,0:T(8,128)(2,1)}, f32[4,768,128]{2,1,0:T(8,128)}) custom-call(s32[21]{0:T(128)} %add_add_fusion.2.scal, bf16[3,768,768]{2,1,0:T(8,128)(2,1)} %collective-permute-done.8.rest_0_, bf16[16,2,128,768]{3,2,1,0:T(8,128)(2,1)} %collective-permute-done.9.rest_1_, f32[2,768,128]{2,1,0:T(8,128)} %pad_maximum_fusion.2.rest_2_), custom_call_target="tpu_custom_call" | custom-call | flops 17716740096 | bytes 8388608 | tf_op jit(solution)/shard_map/attend_new/pallas_call | solution.py:284
  405.6 0.9 copy-done.8
  406.4 15.6 %attend_prefix.5 = bf16[768,384]{1,0:T(8,128)(2,1)} custom-call(s32[21]{0:T(128)} %concatenate.46.scal, bf16[4,768,128]{2,1,0:T(8,128)(2,1)} %get-tuple-element.41.rest_0_, f32[4,768,128]{2,1,0:T(8,128)} %get-tuple-element.42.rest_1_, bf16[2,256,768]{2,1,0:T(8,128)(2,1)} %copy-done.3, bf16[2,256,768]{2,1,0:T(8,128)(2,1)} %copy-done.5, ...), custom_call_target="tpu_custom_call" | custom-call | flops 12884901888 | bytes 8388608 | tf_op jit(solution)/shard_map/attend_prefix/pallas_call | solution.py:284
  422.1 1.2 slice.41
  423.3 1.5 collective-permute-start.15
  424.8 7.2 %collective-permute-start.14 = (bf16[768,384]{1,0:T(8,128)(2,1)}, bf16[768,384]{1,0:T(8,128)(2,1)S(1)}, u32[]{:S(2)}, u32[]{:S(2)}) collective-permute-start(bf16[768,384]{1,0:T(8,128)(2,1)} %attend_prefix.5), channel_id=1, source_target_pairs={{0,2},{2,0},{4,6},{6,4},{8,10},{10,8},{12,14},{14,12},{16,18},{18,... | collective-permute-start | bytes 1769480 | tf_op jit(solution)/shard_map/ppermute | solution.py:397
  432.0 15.6 %attend_prefix.4 = bf16[768,384]{1,0:T(8,128)(2,1)} custom-call(s32[21]{0:T(128)} %get-tuple-element.54.scal, bf16[4,768,128]{2,1,0:T(8,128)(2,1)} %get-tuple-element.38.rest_0_, f32[4,768,128]{2,1,0:T(8,128)} %get-tuple-element.39.rest_1_, bf16[2,256,768]{2,1,0:T(8,128)(2,1)} %copy-done.3, bf16[2,256,768]{2,1,0:T(8,128)(2,1)} %copy-done.5, ...), custom_call_target="tpu_custom_call" | custom-call | flops 12884901888 | bytes 8388608 | tf_op jit(solution)/shard_map/attend_prefix/pallas_call | solution.py:284
  447.6 1.2 slice.40
  451.1 15.9 %attend_prefix.7.rest_6_ = bf16[768,384]{1,0:T(8,128)(2,1)} custom-call(s32[21]{0:T(128)} %add_add_fusion.3.scal, bf16[4,768,128]{2,1,0:T(8,128)(2,1)} %get-tuple-element.45.rest_0_, f32[4,768,128]{2,1,0:T(8,128)} %get-tuple-element.46.rest_1_, bf16[2,256,768]{2,1,0:T(8,128)(2,1)} %copy-done.3, bf16[2,256,768]{2,1,0:T(8,128)(2,1)} %copy-done.5, ...), custom_call_target="tpu_custom_call" | custom-call | flops 12884901888 | bytes 8388608 | tf_op jit(solution)/shard_map/attend_prefix/pallas_call | solution.py:284
  467.1 1.6 collective-permute-start.18
  469.2 15.6 %attend_prefix.6.rest_4_ = bf16[768,384]{1,0:T(8,128)(2,1)} custom-call(s32[21]{0:T(128)} %add_add_fusion.4.scal, bf16[4,768,128]{2,1,0:T(8,128)(2,1)} %get-tuple-element.43.rest_0_, f32[4,768,128]{2,1,0:T(8,128)} %get-tuple-element.44.rest_1_, bf16[2,256,768]{2,1,0:T(8,128)(2,1)} %copy-done.3, bf16[2,256,768]{2,1,0:T(8,128)(2,1)} %copy-done.5, ...), custom_call_target="tpu_custom_call" | custom-call | flops 12884901888 | bytes 8388608 | tf_op jit(solution)/shard_map/attend_prefix/pallas_call | solution.py:284
  486.0 14.6 %collective-permute-done.17.rest_5_ = bf16[768,384]{1,0:T(8,128)(2,1)S(1)} collective-permute-done((bf16[768,384]{1,0:T(8,128)(2,1)}, bf16[768,384]{1,0:T(8,128)(2,1)S(1)}, u32[]{:S(2)}, u32[]{:S(2)}) %collective-permute-start.17) | collective-permute-done | bytes 589856 | tf_op jit(solution)/shard_map/ppermute | solution.py:434
  500.6 1.1 copy-done.1
  501.7 19.3 %project.1 = bf16[768,3072]{1,0:T(8,128)(2,1)} custom-call(s32[9]{0:T(128)S(1)} %stack.57.scal, bf16[768,384]{1,0:T(8,128)(2,1)S(1)} %collective-permute-done.11.rest_0_, bf16[768,384]{1,0:T(8,128)(2,1)} %collective-permute-done.13.rest_1_, bf16[768,384]{1,0:T(8,128)(2,1)S(1)} %collective-permute-done.14.rest_2_, ...), custom_call_target="tpu_custom_call" | custom-call | flops 14495514624 | bytes 28311552 | tf_op jit(solution)/shard_map/project/pallas_call | solution.py:325
  (60 shorter events, 5.5 us)
Async XLA Ops:
  1.2 7.3 %collective-permute-start.1 = (bf16[2,128,768]{2,1,0:T(8,128)(2,1)S(1)}, bf16[2,128,768]{2,1,0:T(8,128)(2,1)S(1)}, u32[]{:S(2)}, u32[]{:S(2)}) collective-permute-start(bf16[2,128,768]{2,1,0:T(8,128)(2,1)S(1)} %get-tuple-element.48), channel_id=1, source_target_pairs={{0,2},{2,0},{4,6},{6,4},{8,10},{10,8},{12,14},{14,12},{16,18},{18,... | collective-permute-start | bytes 1179656 | tf_op jit(solution)/shard_map/ppermute | solution.py:397
  3.3 1.3 collective-permute-start
  10.2 290.2 %copy-start.4 = (s32[1,16]{1,0:T(1,128)S(1)}, s32[1,16]{1,0:T(1,128)}, u32[]{:S(2)}) copy-start(s32[1,16]{1,0:T(1,128)} %param.11) | copy-start | bytes 196
  252.8 101.1 %collective-permute-start.9 = (bf16[16,2,128,768]{3,2,1,0:T(8,128)(2,1)}, bf16[16,2,128,768]{3,2,1,0:T(8,128)(2,1)}, u32[]{:S(2)}, u32[]{:S(2)}) collective-permute-start(bf16[16,2,128,768]{3,2,1,0:T(8,128)(2,1)} %get-tuple-element.35), channel_id=1, source_target_pairs={{0,2},{2,0},{4,6},{6,4},{8,10},{10,8},{12,14},{14,12},{16,18},{18,... | collective-permute-start | bytes 18874376 | tf_op jit(solution)/shard_map/ppermute | solution.py:397
  252.8 101.0 %collective-permute-start.8 = (bf16[3,768,768]{2,1,0:T(8,128)(2,1)}, bf16[3,768,768]{2,1,0:T(8,128)(2,1)}, u32[]{:S(2)}, u32[]{:S(2)}) collective-permute-start(bf16[3,768,768]{2,1,0:T(8,128)(2,1)} %get-tuple-element.34), channel_id=1, source_target_pairs={{0,2},{2,0},{4,6},{6,4},{8,10},{10,8},{12,14},{14,12},{16,18},{18,... | collective-permute-start | bytes 10616840 | tf_op jit(solution)/shard_map/ppermute | solution.py:397
  253.4 92.0 %copy-start.3 = (bf16[2,256,768]{2,1,0:T(8,128)(2,1)}, bf16[2,256,768]{2,1,0:T(8,128)(2,1)S(1)}, u32[]{:S(2)}) copy-start(bf16[2,256,768]{2,1,0:T(8,128)(2,1)S(1)} %pad_maximum_fusion.rest_2_) | copy-start | bytes 2359300
  253.4 64.8 %collective-permute-start.2 = (bf16[2,256,768]{2,1,0:T(8,128)(2,1)S(1)}, bf16[2,256,768]{2,1,0:T(8,128)(2,1)S(1)}, u32[]{:S(2)}, u32[]{:S(2)}) collective-permute-start(bf16[2,256,768]{2,1,0:T(8,128)(2,1)S(1)} %pad_maximum_fusion.rest_2_), channel_id=1, source_target_pairs={{0,8},{2,10},{8,16},{10,18},{16,24},{18,26},{24,28},{26,30},{28,20... | collective-permute-start | bytes 2359304 | tf_op jit(solution)/shard_map/ppermute | solution.py:404
  290.6 27.5 %collective-permute-start.3 = (bf16[2,256,768]{2,1,0:T(8,128)(2,1)S(1)}, bf16[2,256,768]{2,1,0:T(8,128)(2,1)}, u32[]{:S(2)}, u32[]{:S(2)}) collective-permute-start(bf16[2,256,768]{2,1,0:T(8,128)(2,1)S(1)} %pad_maximum_fusion.rest_2_), channel_id=1, source_target_pairs={{8,0},{10,2},{16,8},{18,10},{24,16},{26,18},{28,24},{30,26},{20,28... | collective-permute-start | bytes 2359304 | tf_op jit(solution)/shard_map/ppermute | solution.py:404
  318.1 27.3 %copy-start.5 = (bf16[2,256,768]{2,1,0:T(8,128)(2,1)}, bf16[2,256,768]{2,1,0:T(8,128)(2,1)S(1)}, u32[]{:S(2)}) copy-start(bf16[2,256,768]{2,1,0:T(8,128)(2,1)S(1)} %collective-permute-done.2.rest_3_) | copy-start | bytes 2359300
  318.2 30.3 %collective-permute-start.4 = (bf16[2,256,768]{2,1,0:T(8,128)(2,1)S(1)}, bf16[2,256,768]{2,1,0:T(8,128)(2,1)}, u32[]{:S(2)}, u32[]{:S(2)}) collective-permute-start(bf16[2,256,768]{2,1,0:T(8,128)(2,1)S(1)} %collective-permute-done.2.rest_3_), channel_id=1, source_target_pairs={{0,8},{2,10},{8,16},{10,18},{16,24},{18,26},{24,28},{26,30},{28,20... | collective-permute-start | bytes 2359304 | tf_op jit(solution)/shard_map/ppermute | solution.py:422
  318.2 30.3 %collective-permute-start.5 = (bf16[2,256,768]{2,1,0:T(8,128)(2,1)}, bf16[2,256,768]{2,1,0:T(8,128)(2,1)}, u32[]{:S(2)}, u32[]{:S(2)}) collective-permute-start(bf16[2,256,768]{2,1,0:T(8,128)(2,1)} %collective-permute-done.3.rest_4_), channel_id=1, source_target_pairs={{8,0},{10,2},{16,8},{18,10},{24,16},{26,18},{28,24},{30,26},{20,28... | collective-permute-start | bytes 2359304 | tf_op jit(solution)/shard_map/ppermute | solution.py:424
  348.5 30.8 %collective-permute-start.6 = (bf16[2,256,768]{2,1,0:T(8,128)(2,1)}, bf16[2,256,768]{2,1,0:T(8,128)(2,1)S(1)}, u32[]{:S(2)}, u32[]{:S(2)}) collective-permute-start(bf16[2,256,768]{2,1,0:T(8,128)(2,1)} %collective-permute-done.4.rest_5_), channel_id=1, source_target_pairs={{0,8},{2,10},{8,16},{10,18},{16,24},{18,26},{24,28},{26,30},{28,20... | collective-permute-start | bytes 2359304 | tf_op jit(solution)/shard_map/ppermute | solution.py:422
  353.8 25.5 %collective-permute-start.7 = (bf16[2,256,768]{2,1,0:T(8,128)(2,1)}, bf16[2,256,768]{2,1,0:T(8,128)(2,1)S(1)}, u32[]{:S(2)}, u32[]{:S(2)}) collective-permute-start(bf16[2,256,768]{2,1,0:T(8,128)(2,1)} %collective-permute-done.5.rest_6_), channel_id=1, source_target_pairs={{8,0},{10,2},{16,8},{18,10},{24,16},{26,18},{28,24},{30,26},{20,28... | collective-permute-start | bytes 2359304 | tf_op jit(solution)/shard_map/ppermute | solution.py:424
  379.3 26.2 %copy-start.6 = (bf16[2,256,768]{2,1,0:T(8,128)(2,1)}, bf16[2,256,768]{2,1,0:T(8,128)(2,1)S(1)}, u32[]{:S(2)}) copy-start(bf16[2,256,768]{2,1,0:T(8,128)(2,1)S(1)} %collective-permute-done.6.rest_7_) | copy-start | bytes 2359300
  379.3 26.2 %copy-start.7 = (bf16[2,256,768]{2,1,0:T(8,128)(2,1)}, bf16[2,256,768]{2,1,0:T(8,128)(2,1)S(1)}, u32[]{:S(2)}) copy-start(bf16[2,256,768]{2,1,0:T(8,128)(2,1)S(1)} %collective-permute-done.7.rest_8_) | copy-start | bytes 2359300
  379.3 26.2 %collective-permute-start.10 = (bf16[2,256,768]{2,1,0:T(8,128)(2,1)S(1)}, bf16[2,256,768]{2,1,0:T(8,128)(2,1)S(1)}, u32[]{:S(2)}, u32[]{:S(2)}) collective-permute-start(bf16[2,256,768]{2,1,0:T(8,128)(2,1)S(1)} %collective-permute-done.6.rest_7_), channel_id=1, source_target_pairs={{0,8},{2,10},{8,16},{10,18},{16,24},{18,26},{24,28},{26,30},{28,20... | collective-permute-start | bytes 2359304 | tf_op jit(solution)/shard_map/ppermute | solution.py:422
  405.5 0.9 copy-start.8
  423.3 62.1 %collective-permute-start.15 = (bf16[768,384]{1,0:T(8,128)(2,1)}, bf16[768,384]{1,0:T(8,128)(2,1)}, u32[]{:S(2)}, u32[]{:S(2)}) collective-permute-start(bf16[768,384]{1,0:T(8,128)(2,1)} %attend_prefix.5), channel_id=1, source_target_pairs={{0,1},{1,0},{2,3},{3,2},{4,5},{5,4},{6,7},{7,6},{8,9},{9,8},{10,11... | collective-permute-start | bytes 1769480 | tf_op jit(solution)/shard_map/ppermute | solution.py:434
  424.8 75.8 %collective-permute-start.14 = (bf16[768,384]{1,0:T(8,128)(2,1)}, bf16[768,384]{1,0:T(8,128)(2,1)S(1)}, u32[]{:S(2)}, u32[]{:S(2)}) collective-permute-start(bf16[768,384]{1,0:T(8,128)(2,1)} %attend_prefix.5), channel_id=1, source_target_pairs={{0,2},{2,0},{4,6},{6,4},{8,10},{10,8},{12,14},{14,12},{16,18},{18,... | collective-permute-start | bytes 1769480 | tf_op jit(solution)/shard_map/ppermute | solution.py:397
  448.8 36.6 %collective-permute-start.12 = (bf16[768,384]{1,0:T(8,128)(2,1)}, bf16[768,384]{1,0:T(8,128)(2,1)}, u32[]{:S(2)}, u32[]{:S(2)}) collective-permute-start(bf16[768,384]{1,0:T(8,128)(2,1)} %attend_prefix.4), channel_id=1, source_target_pairs={{0,1},{1,0},{2,3},{3,2},{4,5},{5,4},{6,7},{7,6},{8,9},{9,8},{10,11... | collective-permute-start | bytes 1769480 | tf_op jit(solution)/shard_map/ppermute | solution.py:434
  449.3 51.3 %collective-permute-start.11 = (bf16[768,384]{1,0:T(8,128)(2,1)}, bf16[768,384]{1,0:T(8,128)(2,1)S(1)}, u32[]{:S(2)}, u32[]{:S(2)}) collective-permute-start(bf16[768,384]{1,0:T(8,128)(2,1)} %attend_prefix.4), channel_id=1, source_target_pairs={{0,2},{2,0},{4,6},{6,4},{8,10},{10,8},{12,14},{14,12},{16,18},{18,... | collective-permute-start | bytes 1769480 | tf_op jit(solution)/shard_map/ppermute | solution.py:397
  467.1 17.8 %collective-permute-start.18 = (bf16[768,384]{1,0:T(8,128)(2,1)}, bf16[768,384]{1,0:T(8,128)(2,1)S(1)}, u32[]{:S(2)}, u32[]{:S(2)}) collective-permute-start(bf16[768,384]{1,0:T(8,128)(2,1)} %attend_prefix.7.rest_6_), channel_id=1, source_target_pairs={{0,1},{1,0},{2,3},{3,2},{4,5},{5,4},{6,7},{7,6},{8,9},{9,8},{10,11... | collective-permute-start | bytes 1769480 | tf_op jit(solution)/shard_map/ppermute | solution.py:434
  469.2 31.4 %copy-start = (bf16[768,384]{1,0:T(8,128)(2,1)S(1)}, bf16[768,384]{1,0:T(8,128)(2,1)}, u32[]{:S(2)}) copy-start(bf16[768,384]{1,0:T(8,128)(2,1)} %attend_prefix.7.rest_6_) | copy-start | bytes 1769476
  469.2 31.4 %copy-start.2 = (f32[3072]{0:T(1024)S(1)}, f32[3072]{0:T(1024)}, u32[]{:S(2)}) copy-start(f32[3072]{0:T(1024)} %param.15) | copy-start | bytes 36868
  484.8 15.7 %collective-permute-start.17 = (bf16[768,384]{1,0:T(8,128)(2,1)}, bf16[768,384]{1,0:T(8,128)(2,1)S(1)}, u32[]{:S(2)}, u32[]{:S(2)}) collective-permute-start(bf16[768,384]{1,0:T(8,128)(2,1)} %attend_prefix.6.rest_4_), channel_id=1, source_target_pairs={{0,1},{1,0},{2,3},{3,2},{4,5},{5,4},{6,7},{7,6},{8,9},{9,8},{10,11... | collective-permute-start | bytes 1769480 | tf_op jit(solution)/shard_map/ppermute | solution.py:434
  485.4 15.2 %collective-permute-start.16 = (bf16[768,384]{1,0:T(8,128)(2,1)}, bf16[768,384]{1,0:T(8,128)(2,1)S(1)}, u32[]{:S(2)}, u32[]{:S(2)}) collective-permute-start(bf16[768,384]{1,0:T(8,128)(2,1)} %collective-permute-done.15), channel_id=1, source_target_pairs={{0,2},{2,0},{4,6},{6,4},{8,10},{10,8},{12,14},{14,12},{16,18},{18,... | collective-permute-start | bytes 1769480 | tf_op jit(solution)/shard_map/ppermute | solution.py:397
  485.4 15.2 %collective-permute-start.13 = (bf16[768,384]{1,0:T(8,128)(2,1)}, bf16[768,384]{1,0:T(8,128)(2,1)}, u32[]{:S(2)}, u32[]{:S(2)}) collective-permute-start(bf16[768,384]{1,0:T(8,128)(2,1)} %collective-permute-done.12), channel_id=1, source_target_pairs={{0,2},{2,0},{4,6},{6,4},{8,10},{10,8},{12,14},{14,12},{16,18},{18,... | collective-permute-start | bytes 1769480 | tf_op jit(solution)/shard_map/ppermute | solution.py:397
  500.6 1.1 copy-start.1
where the time goes:
time: 532 us; the launch traced here: 521 us
  Pallas kernels  401 us (75%)
  starting transfers between devices  67.5 us (13%)
  waiting for transfers between devices  31.5 us (6%)
  other arithmetic  8.66 us (2%)
  local copies, waits for them, and re-layouts  8.45 us (2%)
    pallas_call x8, Pallas kernels, attend(): pl.pallas_call(functools.partial(attend_kernel, local=bool(local), prefix...  382 us
    ppermute x1, starting transfers between devices, local_fn(): lax.ppermute(mine, 'tok', ahead)  37.2 us
    pallas_call x1, Pallas kernels, project(): pl.pallas_call(functools.partial(project_kernel, n=n, bq=math.gcd(span, 2...  19.3 us
    ppermute x1, waiting for transfers between devices, local_fn(): lax.ppermute(mine, 'tok', ahead)  16.9 us
    ppermute x4, waiting for transfers between devices, local_fn(): far = lax.ppermute(got, 'fsdp', ypairs)  14.6 us
  transfers between devices with their start and end apart: 19, of which 2 were waited for; matrix products, arithmetic and copies ran while one was open for 2% of the time, Pallas kernels for 24%

commit v1 on v0

--- a/solution.py
+++ b/solution.py
@@ -49,7 +49,7 @@
             qkv_out, pool_out = next(it), next(it)
         qk, sem_q, sem_c = next(it), next(it), next(it)
         if send:
-            sem_s, sem_t = next(it), next(it)
+            qkv_held, pool_held, sem_s, sem_t = next(it), next(it), next(it), next(it)
     kb, vb, kh, vh = next(it), next(it), next(it), next(it)
     if prefix:
         sem_p = next(it)
@@ -98,17 +98,31 @@
 
         if send:
             scol = pl.ds(pl.multiple_of(scal[4], LANES), qkv_out.shape[2])
-            qkv_send = pltpu.make_async_copy(qkv.at[:, :, scol], qkv_out, sem_s)
-            qkv_send.start()
-
-            def page_send(g):
+            qkv_take = pltpu.make_async_copy(qkv.at[:, :, scol], qkv_held, sem_s)
+            qkv_give = pltpu.make_async_copy(qkv_held, qkv_out, sem_s)
+
+            def page_take(g):
                 page = scal[HEAD + g]
-                return pltpu.make_async_copy(pool.at[page, :, :, scol], pool_out.at[page], sem_t.at[g])
-
-            def start_send(g, c):
-                page_send(g).start()
+                return pltpu.make_async_copy(pool.at[page, :, :, scol], pool_held.at[g], sem_t.at[g])
+
+            def page_give(g):
+                page = scal[HEAD + g]
+                return pltpu.make_async_copy(pool_held.at[g], pool_out.at[page], sem_t.at[g])
+
+            def take(g, c):
+                page_take(g).start()
                 return c
-            lax.fori_loop(0, n_pages, start_send, 0)
+
+            def give(g, c):
+                page_take(g).wait()
+                page_give(g).start()
+                return c
+
+            def gone(g, c):
+                page_give(g).wait()
+                return c
+            qkv_take.start()
+            lax.fori_loop(0, n_pages, take, 0)
 
     def piece_copies(i):
         at, n = piece[i]
@@ -169,6 +183,10 @@
                     vh[h, pl.ds(at, page_len), :] = zero
             return c
         lax.fori_loop(0, n_cb * per, prep_page, 0)
+        if send:
+            qkv_take.wait()
+            qkv_give.start()
+            lax.fori_loop(0, n_pages, give, 0)
 
     if prefix:
         for i in range(len(piece)):
@@ -230,11 +248,8 @@
     lax.fori_loop(0, pl.cdiv(live, bq), tile, 0)
 
     if send:
-        def wait_send(g, c):
-            page_send(g).wait()
-            return c
-        qkv_send.wait()
-        lax.fori_loop(0, n_pages, wait_send, 0)
+        qkv_give.wait()
+        lax.fori_loop(0, n_pages, gone, 0)
 
 
 def attend(scal, span, page_len, max_pages, local=None, carry=None, pieces=None, send=0, bq=256):
@@ -277,7 +292,8 @@
             pltpu.SemaphoreType.DMA((2, max_pages)),
         ]
         if send:
-            scratch += [pltpu.SemaphoreType.DMA, pltpu.SemaphoreType.DMA((max_pages,))]
+            scratch += [pltpu.VMEM((3, span, send), bf16), pltpu.VMEM((max_pages, 2, page_len, send), bf16),
+                        pltpu.SemaphoreType.DMA, pltpu.SemaphoreType.DMA((max_pages,))]
     scratch += [pltpu.VMEM((keys, GW), bf16)] * 2 + [pltpu.VMEM((GROUP, keys, LANES), bf16)] * 2
     if pieces:
         scratch += [pltpu.SemaphoreType.DMA((2, len(pieces)))]

time: 532 us -> 256 us (0.48)
  the two profiles are of different devices: /device:TPU:8 before, /device:TPU:0 now
where the time goes in v1:
time: 256 us; the launch traced here: 251 us
  Pallas kernels  184 us (72%)
  waiting for transfers between devices  31.5 us (12%)
  starting transfers between devices  14.6 us (6%)
  other arithmetic  8.66 us (3%)
  local copies, waits for them, and re-layouts  8.45 us (3%)
  between operations  4.01 us (2%)
    pallas_call x8, Pallas kernels, attend(): pl.pallas_call(functools.partial(attend_kernel, local=bool(local), prefix...  165 us
    pallas_call x1, Pallas kernels, project(): pl.pallas_call(functools.partial(project_kernel, n=n, bq=math.gcd(span, 2...  19.3 us
    ppermute x1, waiting for transfers between devices, local_fn(): lax.ppermute(mine, 'tok', ahead)  16.9 us
    ppermute x4, waiting for transfers between devices, local_fn(): far = lax.ppermute(got, 'fsdp', ypairs)  14.3 us
  transfers between devices with their start and end apart: 19, of which 3 were waited for; matrix products, arithmetic and copies ran while one was open for 5% of the time, Pallas kernels for 49%

profile of v1, /device:TPU:0, one launch (start us, length us, event | category | flops | bytes accessed | tf_op | source)
XLA Modules:
  0.0 251.5 jit_solution(12208531365191603913)
XLA Ops:
  0.0 1.2 constant_dynamic-slice_fusion.1
  3.0 0.7 pad_add_fusion
  3.9 0.7 concatenate.42
  4.9 2.8 %multiply_cosine_fusion.1 = (f32[1,768,128]{2,1,0:T(8,128)S(1)}, f32[1,768,128]{2,1,0:T(8,128)S(1)}, f32[1,768,128]{2,1,0:T(8,128)S(1)}, f32[1,768,128]{2,1,0:T(8,128)S(1)}) fusion(f32[128]{0:T(128)S(1)} %get-tuple-element.60, f32[768]{0:T(1024)S(1)} %get-tuple-element.58, f32[128]{0:T(128)S(1)} %get-tuple-element.59, f32[768]{0:T(1024)S(1)} %get-tuple-element.57), kind=kLoop, calls=%fused_computation.6 | loop fusion | flops 393216 | bytes 1580032 | tf_op jit(solution)/shard_map/cos | solution.py:363
  7.7 1.0 pad_maximum_fusion.1.rest_2_
  9.9 0.6 broadcast_add_fusion.scal
  10.5 25.5 %attend_new.4 = (bf16[4,768,128]{2,1,0:T(8,128)(2,1)}, f32[4,768,128]{2,1,0:T(8,128)}, bf16[3,768,768]{2,1,0:T(8,128)(2,1)}, bf16[16,2,128,768]{3,2,1,0:T(8,128)(2,1)}) custom-call(s32[21]{0:T(128)} %broadcast_add_fusion.scal, bf16[3,768,1536]{2,1,0:T(8,128)(2,1)} %bitcast.34, bf16[16,2,128,1536]{3,2,1,0:T(8,128)(2,1)} %bitcast.32, ...), custom_call_target="tpu_custom_call" | custom-call | flops 17716740096 | bytes 8388608 | tf_op jit(solution)/shard_map/attend_new/pallas_call | solution.py:300
  36.7 2.6 %collective-permute-start.3 = (bf16[2,256,768]{2,1,0:T(8,128)(2,1)S(1)}, bf16[2,256,768]{2,1,0:T(8,128)(2,1)}, u32[]{:S(2)}, u32[]{:S(2)}) collective-permute-start(bf16[2,256,768]{2,1,0:T(8,128)(2,1)S(1)} %pad_maximum_fusion.rest_2_), channel_id=1, source_target_pairs={{8,0},{10,2},{16,8},{18,10},{24,16},{26,18},{28,24},{30,26},{20,28... | collective-permute-start | bytes 2359304 | tf_op jit(solution)/shard_map/ppermute | solution.py:420
  39.4 0.7 concatenate.44.scal
  40.1 16.9 %collective-permute-done.2.rest_3_ = bf16[2,256,768]{2,1,0:T(8,128)(2,1)S(1)} collective-permute-done((bf16[2,256,768]{2,1,0:T(8,128)(2,1)S(1)}, bf16[2,256,768]{2,1,0:T(8,128)(2,1)S(1)}, u32[]{:S(2)}, u32[]{:S(2)}) %collective-permute-start.2) | collective-permute-done | bytes 786464 | tf_op jit(solution)/shard_map/ppermute | solution.py:420
  57.0 3.8 %collective-permute-start.4 = (bf16[2,256,768]{2,1,0:T(8,128)(2,1)S(1)}, bf16[2,256,768]{2,1,0:T(8,128)(2,1)}, u32[]{:S(2)}, u32[]{:S(2)}) collective-permute-start(bf16[2,256,768]{2,1,0:T(8,128)(2,1)S(1)} %collective-permute-done.2.rest_3_), channel_id=1, source_target_pairs={{0,8},{2,10},{8,16},{10,18},{16,24},{18,26},{24,28},{26,30},{28,20... | collective-permute-start | bytes 2359304 | tf_op jit(solution)/shard_map/ppermute | solution.py:438
  60.8 25.4 %attend_new.5 = (bf16[4,768,128]{2,1,0:T(8,128)(2,1)}, f32[4,768,128]{2,1,0:T(8,128)}) custom-call(s32[21]{0:T(128)} %concatenate.44.scal, bf16[3,768,1536]{2,1,0:T(8,128)(2,1)} %bitcast.35, bf16[16,2,128,1536]{3,2,1,0:T(8,128)(2,1)} %bitcast.33, f32[2,768,128]{2,1,0:T(8,128)} %pad_maximum_fusion.1.rest_2_), custom_call_target="tpu_custom_call" | custom-call | flops 17716740096 | bytes 8388608 | tf_op jit(solution)/shard_map/attend_new/pallas_call | solution.py:300
  86.2 0.7 concatenate.46.scal
  86.9 0.7 add_add_fusion.2.scal
  87.6 0.7 add_add_fusion.1
  88.2 1.0 pad_maximum_fusion.2.rest_2_
  89.3 2.0 collective-permute-start.7
  91.3 25.3 %attend_new.6 = (bf16[4,768,128]{2,1,0:T(8,128)(2,1)}, f32[4,768,128]{2,1,0:T(8,128)}) custom-call(s32[21]{0:T(128)} %get-tuple-element.53.scal, bf16[3,768,768]{2,1,0:T(8,128)(2,1)} %collective-permute-done.8.rest_0_, bf16[16,2,128,768]{3,2,1,0:T(8,128)(2,1)} %collective-permute-done.9.rest_1_, f32[2,768,128]{2,1,0:T(8,128)} %pad_maximum_fusion.2.rest_2_), custom_call_target="tpu_custom_call" | custom-call | flops 17716740096 | bytes 8388608 | tf_op jit(solution)/shard_map/attend_new/pallas_call | solution.py:300
  116.7 26.1 %attend_new.7 = (bf16[4,768,128]{2,1,0:T(8,128)(2,1)}, f32[4,768,128]{2,1,0:T(8,128)}) custom-call(s32[21]{0:T(128)} %add_add_fusion.2.scal, bf16[3,768,768]{2,1,0:T(8,128)(2,1)} %collective-permute-done.8.rest_0_, bf16[16,2,128,768]{3,2,1,0:T(8,128)(2,1)} %collective-permute-done.9.rest_1_, f32[2,768,128]{2,1,0:T(8,128)} %pad_maximum_fusion.2.rest_2_), custom_call_target="tpu_custom_call" | custom-call | flops 17716740096 | bytes 8388608 | tf_op jit(solution)/shard_map/attend_new/pallas_call | solution.py:300
  142.8 0.9 copy-done.8
  143.7 15.6 %attend_prefix.5 = bf16[768,384]{1,0:T(8,128)(2,1)} custom-call(s32[21]{0:T(128)} %concatenate.46.scal, bf16[4,768,128]{2,1,0:T(8,128)(2,1)} %get-tuple-element.41.rest_0_, f32[4,768,128]{2,1,0:T(8,128)} %get-tuple-element.42.rest_1_, bf16[2,256,768]{2,1,0:T(8,128)(2,1)} %copy-done.3, bf16[2,256,768]{2,1,0:T(8,128)(2,1)} %copy-done.5, ...), custom_call_target="tpu_custom_call" | custom-call | flops 12884901888 | bytes 8388608 | tf_op jit(solution)/shard_map/attend_prefix/pallas_call | solution.py:300
  159.4 1.2 slice.41
  160.6 1.5 collective-permute-start.15
  162.1 15.6 %attend_prefix.4 = bf16[768,384]{1,0:T(8,128)(2,1)} custom-call(s32[21]{0:T(128)} %get-tuple-element.54.scal, bf16[4,768,128]{2,1,0:T(8,128)(2,1)} %get-tuple-element.38.rest_0_, f32[4,768,128]{2,1,0:T(8,128)} %get-tuple-element.39.rest_1_, bf16[2,256,768]{2,1,0:T(8,128)(2,1)} %copy-done.3, bf16[2,256,768]{2,1,0:T(8,128)(2,1)} %copy-done.5, ...), custom_call_target="tpu_custom_call" | custom-call | flops 12884901888 | bytes 8388608 | tf_op jit(solution)/shard_map/attend_prefix/pallas_call | solution.py:300
  177.7 1.2 slice.40
  181.4 15.9 %attend_prefix.7.rest_6_ = bf16[768,384]{1,0:T(8,128)(2,1)} custom-call(s32[21]{0:T(128)} %add_add_fusion.3.scal, bf16[4,768,128]{2,1,0:T(8,128)(2,1)} %get-tuple-element.45.rest_0_, f32[4,768,128]{2,1,0:T(8,128)} %get-tuple-element.46.rest_1_, bf16[2,256,768]{2,1,0:T(8,128)(2,1)} %copy-done.3, bf16[2,256,768]{2,1,0:T(8,128)(2,1)} %copy-done.5, ...), custom_call_target="tpu_custom_call" | custom-call | flops 12884901888 | bytes 8388608 | tf_op jit(solution)/shard_map/attend_prefix/pallas_call | solution.py:300
  197.4 1.6 collective-permute-start.18
  199.5 15.6 %attend_prefix.6.rest_4_ = bf16[768,384]{1,0:T(8,128)(2,1)} custom-call(s32[21]{0:T(128)} %add_add_fusion.4.scal, bf16[4,768,128]{2,1,0:T(8,128)(2,1)} %get-tuple-element.43.rest_0_, f32[4,768,128]{2,1,0:T(8,128)} %get-tuple-element.44.rest_1_, bf16[2,256,768]{2,1,0:T(8,128)(2,1)} %copy-done.3, bf16[2,256,768]{2,1,0:T(8,128)(2,1)} %copy-done.5, ...), custom_call_target="tpu_custom_call" | custom-call | flops 12884901888 | bytes 8388608 | tf_op jit(solution)/shard_map/attend_prefix/pallas_call | solution.py:300
  215.1 0.6 collective-permute-start.17
  216.3 14.3 %collective-permute-done.17.rest_5_ = bf16[768,384]{1,0:T(8,128)(2,1)S(1)} collective-permute-done((bf16[768,384]{1,0:T(8,128)(2,1)}, bf16[768,384]{1,0:T(8,128)(2,1)S(1)}, u32[]{:S(2)}, u32[]{:S(2)}) %collective-permute-start.17) | collective-permute-done | bytes 589856 | tf_op jit(solution)/shard_map/ppermute | solution.py:450
  230.7 1.1 copy-done.1
  231.8 19.3 %project.1 = bf16[768,3072]{1,0:T(8,128)(2,1)} custom-call(s32[9]{0:T(128)S(1)} %stack.57.scal, bf16[768,384]{1,0:T(8,128)(2,1)S(1)} %collective-permute-done.11.rest_0_, bf16[768,384]{1,0:T(8,128)(2,1)} %collective-permute-done.13.rest_1_, bf16[768,384]{1,0:T(8,128)(2,1)S(1)} %collective-permute-done.14.rest_2_, ...), custom_call_target="tpu_custom_call" | custom-call | flops 14495514624 | bytes 28311552 | tf_op jit(solution)/shard_map/project/pallas_call | solution.py:341
  (60 shorter events, 4.9 us)
Async XLA Ops:
  1.2 7.6 %collective-permute-start.1 = (bf16[2,128,768]{2,1,0:T(8,128)(2,1)S(1)}, bf16[2,128,768]{2,1,0:T(8,128)(2,1)S(1)}, u32[]{:S(2)}, u32[]{:S(2)}) collective-permute-start(bf16[2,128,768]{2,1,0:T(8,128)(2,1)S(1)} %get-tuple-element.48), channel_id=1, source_target_pairs={{0,2},{2,0},{4,6},{6,4},{8,10},{10,8},{12,14},{14,12},{16,18},{18,... | collective-permute-start | bytes 1179656 | tf_op jit(solution)/shard_map/ppermute | solution.py:413
  3.7 1.1 collective-permute-start
  10.5 28.8 %copy-start.4 = (s32[1,16]{1,0:T(1,128)S(1)}, s32[1,16]{1,0:T(1,128)}, u32[]{:S(2)}) copy-start(s32[1,16]{1,0:T(1,128)} %param.11) | copy-start | bytes 196
  35.9 55.3 %collective-permute-start.9 = (bf16[16,2,128,768]{3,2,1,0:T(8,128)(2,1)}, bf16[16,2,128,768]{3,2,1,0:T(8,128)(2,1)}, u32[]{:S(2)}, u32[]{:S(2)}) collective-permute-start(bf16[16,2,128,768]{3,2,1,0:T(8,128)(2,1)} %get-tuple-element.35), channel_id=1, source_target_pairs={{0,2},{2,0},{4,6},{6,4},{8,10},{10,8},{12,14},{14,12},{16,18},{18,... | collective-permute-start | bytes 18874376 | tf_op jit(solution)/shard_map/ppermute | solution.py:413
  36.5 54.8 %collective-permute-start.8 = (bf16[3,768,768]{2,1,0:T(8,128)(2,1)}, bf16[3,768,768]{2,1,0:T(8,128)(2,1)}, u32[]{:S(2)}, u32[]{:S(2)}) collective-permute-start(bf16[3,768,768]{2,1,0:T(8,128)(2,1)} %get-tuple-element.34), channel_id=1, source_target_pairs={{0,2},{2,0},{4,6},{6,4},{8,10},{10,8},{12,14},{14,12},{16,18},{18,... | collective-permute-start | bytes 10616840 | tf_op jit(solution)/shard_map/ppermute | solution.py:413
  36.6 49.5 %copy-start.3 = (bf16[2,256,768]{2,1,0:T(8,128)(2,1)}, bf16[2,256,768]{2,1,0:T(8,128)(2,1)S(1)}, u32[]{:S(2)}) copy-start(bf16[2,256,768]{2,1,0:T(8,128)(2,1)S(1)} %pad_maximum_fusion.rest_2_) | copy-start | bytes 2359300
  36.7 20.3 %collective-permute-start.2 = (bf16[2,256,768]{2,1,0:T(8,128)(2,1)S(1)}, bf16[2,256,768]{2,1,0:T(8,128)(2,1)S(1)}, u32[]{:S(2)}, u32[]{:S(2)}) collective-permute-start(bf16[2,256,768]{2,1,0:T(8,128)(2,1)S(1)} %pad_maximum_fusion.rest_2_), channel_id=1, source_target_pairs={{0,8},{2,10},{8,16},{10,18},{16,24},{18,26},{24,28},{26,30},{28,20... | collective-permute-start | bytes 2359304 | tf_op jit(solution)/shard_map/ppermute | solution.py:420
  36.7 20.3 %collective-permute-start.3 = (bf16[2,256,768]{2,1,0:T(8,128)(2,1)S(1)}, bf16[2,256,768]{2,1,0:T(8,128)(2,1)}, u32[]{:S(2)}, u32[]{:S(2)}) collective-permute-start(bf16[2,256,768]{2,1,0:T(8,128)(2,1)S(1)} %pad_maximum_fusion.rest_2_), channel_id=1, source_target_pairs={{8,0},{10,2},{16,8},{18,10},{24,16},{26,18},{28,24},{30,26},{20,28... | collective-permute-start | bytes 2359304 | tf_op jit(solution)/shard_map/ppermute | solution.py:420
  57.0 29.2 %copy-start.5 = (bf16[2,256,768]{2,1,0:T(8,128)(2,1)}, bf16[2,256,768]{2,1,0:T(8,128)(2,1)S(1)}, u32[]{:S(2)}) copy-start(bf16[2,256,768]{2,1,0:T(8,128)(2,1)S(1)} %collective-permute-done.2.rest_3_) | copy-start | bytes 2359300
  57.0 32.2 %collective-permute-start.4 = (bf16[2,256,768]{2,1,0:T(8,128)(2,1)S(1)}, bf16[2,256,768]{2,1,0:T(8,128)(2,1)}, u32[]{:S(2)}, u32[]{:S(2)}) collective-permute-start(bf16[2,256,768]{2,1,0:T(8,128)(2,1)S(1)} %collective-permute-done.2.rest_3_), channel_id=1, source_target_pairs={{0,8},{2,10},{8,16},{10,18},{16,24},{18,26},{24,28},{26,30},{28,20... | collective-permute-start | bytes 2359304 | tf_op jit(solution)/shard_map/ppermute | solution.py:438
  60.8 28.5 %collective-permute-start.5 = (bf16[2,256,768]{2,1,0:T(8,128)(2,1)}, bf16[2,256,768]{2,1,0:T(8,128)(2,1)}, u32[]{:S(2)}, u32[]{:S(2)}) collective-permute-start(bf16[2,256,768]{2,1,0:T(8,128)(2,1)} %collective-permute-done.3.rest_4_), channel_id=1, source_target_pairs={{8,0},{10,2},{16,8},{18,10},{24,16},{26,18},{28,24},{30,26},{20,28... | collective-permute-start | bytes 2359304 | tf_op jit(solution)/shard_map/ppermute | solution.py:440
  89.2 27.4 %collective-permute-start.6 = (bf16[2,256,768]{2,1,0:T(8,128)(2,1)}, bf16[2,256,768]{2,1,0:T(8,128)(2,1)S(1)}, u32[]{:S(2)}, u32[]{:S(2)}) collective-permute-start(bf16[2,256,768]{2,1,0:T(8,128)(2,1)} %collective-permute-done.4.rest_5_), channel_id=1, source_target_pairs={{0,8},{2,10},{8,16},{10,18},{16,24},{18,26},{24,28},{26,30},{28,20... | collective-permute-start | bytes 2359304 | tf_op jit(solution)/shard_map/ppermute | solution.py:438
  89.3 27.4 %collective-permute-start.7 = (bf16[2,256,768]{2,1,0:T(8,128)(2,1)}, bf16[2,256,768]{2,1,0:T(8,128)(2,1)S(1)}, u32[]{:S(2)}, u32[]{:S(2)}) collective-permute-start(bf16[2,256,768]{2,1,0:T(8,128)(2,1)} %collective-permute-done.5.rest_6_), channel_id=1, source_target_pairs={{8,0},{10,2},{16,8},{18,10},{24,16},{26,18},{28,24},{30,26},{20,28... | collective-permute-start | bytes 2359304 | tf_op jit(solution)/shard_map/ppermute | solution.py:440
  116.6 26.2 %copy-start.6 = (bf16[2,256,768]{2,1,0:T(8,128)(2,1)}, bf16[2,256,768]{2,1,0:T(8,128)(2,1)S(1)}, u32[]{:S(2)}) copy-start(bf16[2,256,768]{2,1,0:T(8,128)(2,1)S(1)} %collective-permute-done.6.rest_7_) | copy-start | bytes 2359300
  116.7 26.2 %copy-start.7 = (bf16[2,256,768]{2,1,0:T(8,128)(2,1)}, bf16[2,256,768]{2,1,0:T(8,128)(2,1)S(1)}, u32[]{:S(2)}) copy-start(bf16[2,256,768]{2,1,0:T(8,128)(2,1)S(1)} %collective-permute-done.7.rest_8_) | copy-start | bytes 2359300
  116.7 26.2 %collective-permute-start.10 = (bf16[2,256,768]{2,1,0:T(8,128)(2,1)S(1)}, bf16[2,256,768]{2,1,0:T(8,128)(2,1)S(1)}, u32[]{:S(2)}, u32[]{:S(2)}) collective-permute-start(bf16[2,256,768]{2,1,0:T(8,128)(2,1)S(1)} %collective-permute-done.6.rest_7_), channel_id=1, source_target_pairs={{0,8},{2,10},{8,16},{10,18},{16,24},{18,26},{24,28},{26,30},{28,20... | collective-permute-start | bytes 2359304 | tf_op jit(solution)/shard_map/ppermute | solution.py:438
  142.8 0.9 copy-start.8
  160.6 55.1 %collective-permute-start.15 = (bf16[768,384]{1,0:T(8,128)(2,1)}, bf16[768,384]{1,0:T(8,128)(2,1)}, u32[]{:S(2)}, u32[]{:S(2)}) collective-permute-start(bf16[768,384]{1,0:T(8,128)(2,1)} %attend_prefix.5), channel_id=1, source_target_pairs={{0,1},{1,0},{2,3},{3,2},{4,5},{5,4},{6,7},{7,6},{8,9},{9,8},{10,11... | collective-permute-start | bytes 1769480 | tf_op jit(solution)/shard_map/ppermute | solution.py:450
  162.1 68.6 %collective-permute-start.14 = (bf16[768,384]{1,0:T(8,128)(2,1)}, bf16[768,384]{1,0:T(8,128)(2,1)S(1)}, u32[]{:S(2)}, u32[]{:S(2)}) collective-permute-start(bf16[768,384]{1,0:T(8,128)(2,1)} %attend_prefix.5), channel_id=1, source_target_pairs={{0,2},{2,0},{4,6},{6,4},{8,10},{10,8},{12,14},{14,12},{16,18},{18,... | collective-permute-start | bytes 1769480 | tf_op jit(solution)/shard_map/ppermute | solution.py:413
  178.9 36.8 %collective-permute-start.12 = (bf16[768,384]{1,0:T(8,128)(2,1)}, bf16[768,384]{1,0:T(8,128)(2,1)}, u32[]{:S(2)}, u32[]{:S(2)}) collective-permute-start(bf16[768,384]{1,0:T(8,128)(2,1)} %attend_prefix.4), channel_id=1, source_target_pairs={{0,1},{1,0},{2,3},{3,2},{4,5},{5,4},{6,7},{7,6},{8,9},{9,8},{10,11... | collective-permute-start | bytes 1769480 | tf_op jit(solution)/shard_map/ppermute | solution.py:450
  179.4 51.3 %collective-permute-start.11 = (bf16[768,384]{1,0:T(8,128)(2,1)}, bf16[768,384]{1,0:T(8,128)(2,1)S(1)}, u32[]{:S(2)}, u32[]{:S(2)}) collective-permute-start(bf16[768,384]{1,0:T(8,128)(2,1)} %attend_prefix.4), channel_id=1, source_target_pairs={{0,2},{2,0},{4,6},{6,4},{8,10},{10,8},{12,14},{14,12},{16,18},{18,... | collective-permute-start | bytes 1769480 | tf_op jit(solution)/shard_map/ppermute | solution.py:413
  197.4 17.8 %collective-permute-start.18 = (bf16[768,384]{1,0:T(8,128)(2,1)}, bf16[768,384]{1,0:T(8,128)(2,1)S(1)}, u32[]{:S(2)}, u32[]{:S(2)}) collective-permute-start(bf16[768,384]{1,0:T(8,128)(2,1)} %attend_prefix.7.rest_6_), channel_id=1, source_target_pairs={{0,1},{1,0},{2,3},{3,2},{4,5},{5,4},{6,7},{7,6},{8,9},{9,8},{10,11... | collective-permute-start | bytes 1769480 | tf_op jit(solution)/shard_map/ppermute | solution.py:450
  199.5 31.2 %copy-start = (bf16[768,384]{1,0:T(8,128)(2,1)S(1)}, bf16[768,384]{1,0:T(8,128)(2,1)}, u32[]{:S(2)}) copy-start(bf16[768,384]{1,0:T(8,128)(2,1)} %attend_prefix.7.rest_6_) | copy-start | bytes 1769476
  199.5 31.2 %copy-start.2 = (f32[3072]{0:T(1024)S(1)}, f32[3072]{0:T(1024)}, u32[]{:S(2)}) copy-start(f32[3072]{0:T(1024)} %param.15) | copy-start | bytes 36868
  215.1 15.5 %collective-permute-start.17 = (bf16[768,384]{1,0:T(8,128)(2,1)}, bf16[768,384]{1,0:T(8,128)(2,1)S(1)}, u32[]{:S(2)}, u32[]{:S(2)}) collective-permute-start(bf16[768,384]{1,0:T(8,128)(2,1)} %attend_prefix.6.rest_4_), channel_id=1, source_target_pairs={{0,1},{1,0},{2,3},{3,2},{4,5},{5,4},{6,7},{7,6},{8,9},{9,8},{10,11... | collective-permute-start | bytes 1769480 | tf_op jit(solution)/shard_map/ppermute | solution.py:450
  215.7 14.9 %collective-permute-start.16 = (bf16[768,384]{1,0:T(8,128)(2,1)}, bf16[768,384]{1,0:T(8,128)(2,1)S(1)}, u32[]{:S(2)}, u32[]{:S(2)}) collective-permute-start(bf16[768,384]{1,0:T(8,128)(2,1)} %collective-permute-done.15), channel_id=1, source_target_pairs={{0,2},{2,0},{4,6},{6,4},{8,10},{10,8},{12,14},{14,12},{16,18},{18,... | collective-permute-start | bytes 1769480 | tf_op jit(solution)/shard_map/ppermute | solution.py:413
  215.7 14.9 %collective-permute-start.13 = (bf16[768,384]{1,0:T(8,128)(2,1)}, bf16[768,384]{1,0:T(8,128)(2,1)}, u32[]{:S(2)}, u32[]{:S(2)}) collective-permute-start(bf16[768,384]{1,0:T(8,128)(2,1)} %collective-permute-done.12), channel_id=1, source_target_pairs={{0,2},{2,0},{4,6},{6,4},{8,10},{10,8},{12,14},{14,12},{16,18},{18,... | collective-permute-start | bytes 1769480 | tf_op jit(solution)/shard_map/ppermute | solution.py:413
  230.7 1.1 copy-start.1
